TPU v7x, 32 devices: a whole 2x2x4 slice. The times are simulated.
32 devices in a mesh: parts: 2 (over y), src: 4 (over z), tile: 2 (over x), row: 2 (over core).
Axes of the slice: x: 2, y: 2, z: 4, core: 2. Of those that a mesh axis runs over, the one named last changes fastest.
Arguments:
- mask_windows: float32 [4, 256, 256], P(('parts', 'tile'), ('src', 'row')), parts along dimension 0, may hold values from -4 to 4
- target_windows: float32 [4, 256, 256], P(('parts', 'tile'), ('src', 'row')), parts along dimension 0, may hold values from 0 to 1
- pupil_bands: int32 [24, 128, 2], P(('parts', 'src')), parts along dimension 0, may hold values from 0 to 128, as said below
- pupil_phase: float32 [24, 128, 128], P(('parts', 'src')), parts along dimension 0, may hold values from -3.140625 to 3.140625
- source_weight: float32 [24], P(('parts', 'src')), parts along dimension 0, may hold values from 0.2 to 1
Outputs:
- mask_grad: float32 [4, 256, 256], P(('parts', 'tile'), ('src', 'row')), parts along dimension 0
- source_grad: float32 [24], P(('parts', 'src')), parts along dimension 0
There are 2 independent parts, one for each index of `parts`. A program takes and returns all parts, laid end to end along the dimension named above; each array names one. Nothing has to cross between parts.
Inputs may be any that keep to these rules, and one draw needn't show every extreme that they name: For every source point and frequency row, pupil_bands[s, kx, 0] <= pupil_bands[s, kx, 1]; a row that passes nothing holds (0, 0).
All inputs are finite; a program needn't handle non-finite values.
Results may differ from a plain program's by a relative error of at most 0.00019.
Values sent between devices are 32-bit elements; how exact they have to be, the bound alone decides.
A program may use at most 64 MiB of HBM per device.

v0:
```python
import math
import jax
import jax.numpy as jnp
from jax import lax
from jax.sharding import PartitionSpec as P

M = 256
K = 128
OV = 32
STEEPNESS = 20.0
THRESHOLD = 0.15
LOSS_SCALE = 32.0


def with_halo(block, sides, width):
    for axis, dim in sides:
        count = lax.axis_size(axis)
        forward = [(i, i + 1) for i in range(count - 1)]
        backward = [(target, source) for source, target in forward]
        low = lax.ppermute(
            lax.slice_in_dim(block, block.shape[dim] - width, None, axis=dim), axis, forward
        )
        high = lax.ppermute(lax.slice_in_dim(block, 0, width, axis=dim), axis, backward)
        block = jnp.concatenate([low, block, high], axis=dim)
    return block


def matmul(left_op, right_op):
    return lax.dot_general(
        left_op,
        right_op,
        (((1,), (0,)), ((), ())),
        precision=lax.Precision.HIGHEST,
        preferred_element_type=jnp.float32,
    )


def matmul_tn(left_op, right_op):
    return lax.dot_general(
        left_op,
        right_op,
        (((0,), (0,)), ((), ())),
        precision=lax.Precision.HIGHEST,
        preferred_element_type=jnp.float32,
    )


def matmul_nt(left_op, right_op):
    return lax.dot_general(
        left_op,
        right_op,
        (((1,), (1,)), ((), ())),
        precision=lax.Precision.HIGHEST,
        preferred_element_type=jnp.float32,
    )


def wave_tables(positions):
    freq_index = jnp.arange(K, dtype=jnp.int32) - K // 2
    phase_index = freq_index[:, None] * positions[None, :] % M
    angles = 2.0 * math.pi / M * phase_index.astype(jnp.float32)
    return (jnp.cos(angles), jnp.sin(angles))


def shards(mask_windows, target_windows, pupil_bands, pupil_phase, source_weight):
    src_count = lax.axis_size("src")
    tile_count = lax.axis_size("tile")
    row_count = lax.axis_size("row")
    local_x = mask_windows.shape[1]
    per_device = pupil_phase.shape[0]
    sources = per_device * src_count
    field_scale = 1.0 / (M * K)
    src_id = lax.axis_index("src")
    row_id = lax.axis_index("row")
    x_start = (src_id * row_count + row_id) * local_x
    block_starts = (jnp.arange(src_count, dtype=jnp.int32) * row_count + row_id) * local_x
    row_set = (block_starts[:, None] + jnp.arange(local_x, dtype=jnp.int32)[None, :]).reshape(
        src_count * local_x
    )
    cos_all, sin_all = wave_tables(jnp.arange(M, dtype=jnp.int32))
    cos_set, sin_set = wave_tables(row_set)
    cos_own, sin_own = wave_tables(x_start + jnp.arange(local_x, dtype=jnp.int32))
    window = mask_windows[0]
    goal_block = target_windows[0]
    zero_spec = jnp.zeros((K, K), jnp.float32)
    shard_rows = lax.all_gather(window, ("src", "row"), axis=0, tiled=True)
    part_real = matmul_nt(shard_rows, cos_all)
    part_imag = -matmul_nt(shard_rows, sin_all)
    spec_real = matmul(cos_all, part_real) + matmul(sin_all, part_imag)
    spec_imag = matmul(cos_all, part_imag) - matmul(sin_all, part_real)
    freq_cols = jnp.arange(K, dtype=jnp.int32)
    inside = (freq_cols[None, None, :] >= pupil_bands[:, :, 0:1]) & (
        freq_cols[None, None, :] < pupil_bands[:, :, 1:2]
    )
    passing = inside.astype(jnp.float32)
    pupil_real = passing * jnp.cos(pupil_phase)
    pupil_imag = passing * jnp.sin(pupil_phase)
    amp_real = (pupil_real * spec_real - pupil_imag * spec_imag).reshape(per_device * K, K)
    amp_imag = (pupil_imag * spec_real + pupil_real * spec_imag).reshape(per_device * K, K)
    half_real = (matmul(amp_real, cos_all) - matmul(amp_imag, sin_all)).reshape(per_device, K, M)
    half_imag = (matmul(amp_real, sin_all) + matmul(amp_imag, cos_all)).reshape(per_device, K, M)
    weights = source_weight / sources

    def fields(pair_in):
        one_real, one_imag = pair_in
        field_real = field_scale * (matmul_tn(cos_set, one_real) - matmul_tn(sin_set, one_imag))
        field_imag = field_scale * (matmul_tn(cos_set, one_imag) + matmul_tn(sin_set, one_real))
        return (field_real, field_imag)

    stack_real, stack_imag = lax.map(fields, (half_real, half_imag))
    part_real = stack_real
    part_imag = stack_imag
    intensity = lax.psum_scatter(
        jnp.sum(weights[:, None, None] * (part_real * part_real + part_imag * part_imag), axis=0),
        "src",
        scatter_dimension=0,
        tiled=True,
    )
    resist = jax.nn.sigmoid(STEEPNESS * (intensity - THRESHOLD))
    cotangent = LOSS_SCALE * (resist - goal_block) * STEEPNESS * resist * (1.0 - resist)
    cotangent_all = lax.all_gather(cotangent, "src", axis=0, tiled=True)
    source_ids = jnp.arange(per_device, dtype=jnp.int32)

    def add_back(source_id, totals):
        grad_real, grad_imag, source_terms = totals
        field_real = stack_real[source_id]
        field_imag = stack_imag[source_id]
        back_scale = 2.0 * weights[source_id] * cotangent_all
        back_real = back_scale * field_real
        back_imag = back_scale * field_imag
        adj_real = matmul(cos_set, back_real) + matmul(sin_set, back_imag)
        adj_imag = matmul(cos_set, back_imag) - matmul(sin_set, back_real)
        amp_grad_real = field_scale * (matmul_nt(adj_real, cos_all) + matmul_nt(adj_imag, sin_all))
        amp_grad_imag = field_scale * (matmul_nt(adj_imag, cos_all) - matmul_nt(adj_real, sin_all))
        pass_real = pupil_real[source_id]
        pass_imag = pupil_imag[source_id]
        grad_real = grad_real + pass_real * amp_grad_real + pass_imag * amp_grad_imag
        grad_imag = grad_imag + pass_real * amp_grad_imag - pass_imag * amp_grad_real
        term_value = jnp.sum(cotangent_all * (field_real * field_real + field_imag * field_imag))
        source_terms = source_terms + jnp.where(source_ids == source_id, term_value, 0.0)
        return (grad_real, grad_imag, source_terms)

    grad_real, grad_imag, source_terms = lax.fori_loop(
        0, per_device, add_back, (zero_spec, zero_spec, jnp.zeros((per_device,), jnp.float32))
    )
    grad_real, grad_imag = lax.psum((grad_real, grad_imag), ("src", "row"))
    source_sum = lax.psum(source_terms, ("tile", "row"))
    source_grad = source_sum / (sources * M * tile_count)
    q_one = matmul(grad_real, cos_all) - matmul(grad_imag, sin_all)
    q_two = matmul(grad_real, sin_all) + matmul(grad_imag, cos_all)
    grad_block = matmul_tn(cos_own, q_one) - matmul_tn(sin_own, q_two)
    padded = with_halo(grad_block, (("tile", 1),), OV)
    from_below = padded[:, :OV]
    from_above = padded[:, M + OV :]
    middle = jnp.zeros((local_x, M - 2 * OV), jnp.float32)
    grad_block = grad_block + jnp.concatenate([from_below, middle, from_above], axis=1)
    return (grad_block[None], source_grad)


def solution(mesh):
    return jax.shard_map(
        shards,
        mesh=mesh,
        in_specs=(
            P(("parts", "tile"), ("src", "row"), None),
            P(("parts", "tile"), ("src", "row"), None),
            P(("parts", "src"), None, None),
            P(("parts", "src"), None, None),
            P(("parts", "src")),
        ),
        out_specs=(P(("parts", "tile"), ("src", "row"), None), P(("parts", "src"))),
        check_vma=False,
    )
```

profile of v0, /device:TPU:0, one launch (start us, length us, event | category | flops | bytes accessed | tf_op | source)
XLA Modules:
  0.0 179.0 jit_solution(342020758289789825)
XLA Ops:
  7.2 16.1 %all-gather = f32[1,256,256]{2,1,0:T(8,128)S(1)} all-gather(f32[1,32,256]{2,1,0:T(8,128)} %param.9), channel_id=2, replica_groups=mesh['parts'=2,'src'=4,'tile'=2,'row'=2] {'src','row'}, dimensions={1}, use_global_device_ids=true | all-gather | bytes 294912 | tf_op jit(solution)/shard_map/all_gather | solution.py:86
  23.3 0.9 fusion.123
  24.2 0.9 convolution_negate_fusion
  29.3 1.0 fusion.152
  30.3 1.0 fusion.142
  31.3 1.0 convolution_add_fusion.3
  32.4 1.0 convolution_subtract_fusion.3
  33.6 7.2 %while.35 = (s32[]{:T(128)}, f32[3,128,256]{1,2,0:T(8,128)S(1)}, f32[3,128,256]{1,2,0:T(8,128)S(1)}, f32[3,128,256]{2,1,0:T(8,128)S(1)}, f32[3,128,256]{2,1,0:T(...) while((s32[]{:T(128)}, f32[3,128,256]{1,2,0:T(8,128)S(1)}, ...), condition=%wide.region_1.2_spmd.clone.clone, body=%wide.region_0.1_spmd.clone.clone.sunk | while | flops 202375168 | bytes 1316957 | solution.py:110
  41.9 20.5 %reduce-scatter.4.cloned.1.call-done = f32[32,256]{1,0:T(8,128)} async-done(((f32[128,256]{1,0:T(8,128)}), f32[32,256]{1,0:T(8,128)}) %reduce-scatter.4.cloned.1.call-update) | async-done | bytes 32784 | tf_op jit(solution)/shard_map/reduce_scatter | solution.py:113
  63.1 13.5 %all_gather.7 = f32[128,256]{1,0:T(8,128)S(1)} all-gather(f32[32,256]{1,0:T(8,128)S(1)} %fusion.163), channel_id=1, replica_groups=mesh['parts'=2,'src'=4,'tile'=2,'row'=2] {'src'}, dimensions={0}, use_global_device_ids=true | all-gather | bytes 163840 | tf_op jit(solution)/shard_map/all_gather | solution.py:121
  76.7 26.2 %while.36 = (s32[]{:T(128)}, f32[128,128]{1,0:T(8,128)S(1)}, f32[128,128]{1,0:T(8,128)S(1)}, f32[3]{0:T(128)S(1)}, f32[3,128,128]{2,1,0:T(8,128)S(1)}, /*index=5...) while((s32[]{:T(128)}, f32[128,128]{1,0:T(8,128)S(1)}, ...), condition=%wide.region_6.7_spmd.clone.clone.clone.clone, body=%wide.region_4.6_spmd.clone.clone.clone.clone.sunk | while | flops 406126592 | bytes 4593900 | solution.py:143
  81.5 0.8 fusion.307
  82.3 0.8 fusion.308
  83.2 0.9 fusion.309
  90.2 0.8 fusion.307
  91.9 0.9 fusion.309
  98.9 0.9 fusion.307
  100.7 0.9 fusion.309
  103.5 5.7 %psum.23 = f32[3]{0:T(128)S(1)} all-reduce(f32[3]{0:T(128)S(1)} %get-tuple-element.296), channel_id=1, replica_groups=mesh['parts'=2,'src'=4,'tile'=2,'row'=2] {'tile','row'}, use_global_device_ids=true, to_apply=%region_9.10 | all-reduce | flops 3 | bytes 24 | tf_op jit(solution)/shard_map/psum | solution.py:147
  109.2 47.8 %all-reduce.3.cloned.1.call-done = (f32[128,128]{1,0:T(8,128)}, f32[128,128]{1,0:T(8,128)}) async-done(((f32[128,128]{1,0:T(8,128)}, f32[128,128]{1,0:T(8,128)}), (f32[128,128]{1,0:T(8,128)}, f32[128,128]{1,0:T(8,128)})) %all-reduce.3.cloned.1.call-update) | async-done | bytes 131088 | tf_op jit(solution)/shard_map/psum | solution.py:146
  157.1 1.7 fusion.150
  162.5 3.4 %collective-permute-start = (f32[32,32]{1,0:T(8,128)S(1)}, f32[32,32]{1,0:T(8,128)S(1)}, u32[]{:S(2)}, u32[]{:S(2)}) collective-permute-start(f32[32,32]{1,0:T(8,128)S(1)} %get-tuple-element.617), channel_id=1, source_target_pairs={{0,2},{1,3},{4,6},{5,7},{8,10},{9,11},{12,14},{13,15},{16,18},{17,... | collective-permute-start | bytes 12296 | tf_op jit(solution)/shard_map/ppermute | solution.py:20
  165.9 1.3 collective-permute-start.1
  167.7 3.8 %collective-permute-done.1 = f32[32,32]{1,0:T(8,128)S(1)} collective-permute-done((f32[32,32]{1,0:T(8,128)S(1)}, f32[32,32]{1,0:T(8,128)S(1)}, u32[]{:S(2)}, u32[]{:S(2)}) %collective-permute-start.1) | collective-permute-done | bytes 4128 | tf_op jit(solution)/shard_map/ppermute | solution.py:23
  (100 shorter events, 36.6 us)
Async XLA Ops:
  7.2 55.2 %reduce-scatter.4.cloned.1.call-start = ((), (), s32[]{:S(2)}) async-start(), calls=%async_computation.1 | async-start | bytes 163840 | tf_op jit(solution)/shard_map/reduce_scatter | solution.py:113
  27.5 0.8 copy-start.4
  27.6 0.9 copy-start
  33.6 7.2 %copy-start.7 = (f32[3]{0:T(128)S(1)}, f32[3]{0:T(128)}, u32[]{:S(2)}) copy-start(f32[3]{0:T(128)} %param.13) | copy-start | bytes 40
  41.7 20.7 %copy-start.3 = (f32[1,32,256]{2,1,0:T(8,128)S(1)}, f32[1,32,256]{2,1,0:T(8,128)}, u32[]{:S(2)}) copy-start(f32[1,32,256]{2,1,0:T(8,128)} %param.10) | copy-start | bytes 98308
  41.7 115.4 %all-reduce.3.cloned.1.call-start = ((), (), s32[]{:S(2)}) async-start(), calls=%async_computation.2 | async-start | bytes 262144 | tf_op jit(solution)/shard_map/psum | solution.py:146
  102.8 0.6 copy-start.1
  102.9 0.6 copy-start.2
  157.1 1.7 copy-start.6
  158.8 0.8 copy-start.5
  162.5 5.2 %collective-permute-start = (f32[32,32]{1,0:T(8,128)S(1)}, f32[32,32]{1,0:T(8,128)S(1)}, u32[]{:S(2)}, u32[]{:S(2)}) collective-permute-start(f32[32,32]{1,0:T(8,128)S(1)} %get-tuple-element.617), channel_id=1, source_target_pairs={{0,2},{1,3},{4,6},{5,7},{8,10},{9,11},{12,14},{13,15},{16,18},{17,... | collective-permute-start | bytes 12296 | tf_op jit(solution)/shard_map/ppermute | solution.py:20
  165.9 5.6 %collective-permute-start.1 = (f32[32,32]{1,0:T(8,128)S(1)}, f32[32,32]{1,0:T(8,128)S(1)}, u32[]{:S(2)}, u32[]{:S(2)}) collective-permute-start(f32[32,32]{1,0:T(8,128)S(1)} %get-tuple-element.618), channel_id=1, source_target_pairs={{2,0},{3,1},{6,4},{7,5},{10,8},{11,9},{14,12},{15,13},{18,16},{19,... | collective-permute-start | bytes 12296 | tf_op jit(solution)/shard_map/ppermute | solution.py:23
Sparse Core Ops, SparseCore 0:
  41.8 20.4 reduce-scatter.3
  103.6 53.3 all-reduce.2
where the time goes:
time: 179 us
  waiting for transfers between devices  72.2 us (40%)
  matrix products  39.2 us (22%)
  blocking collectives  35.3 us (20%)
  between operations  14.4 us (8%)
  other arithmetic  6.82 us (4%)
  starting transfers between devices  4.74 us (3%)
  local copies, waits for them, and re-layouts  4.13 us (2%)
  loops' own time  2.33 us (1%)
    psum x1, waiting for transfers between devices, shards(): grad_real, grad_imag = lax.psum((grad_real, grad_imag), ('src', 'row'))  47.8 us
    reduce_scatter x1, waiting for transfers between devices, shards(): lax.psum_scatter(jnp.sum(weights[:, None, None] * (part_real * part_real...  20.5 us
    dot_general x24, matrix products, matmul(): lax.dot_general(left_op, right_op, (((1,), (0,)), ((), ())), precision=la...  18.9 us
    all_gather x1, blocking collectives, shards(): shard_rows = lax.all_gather(window, ('src', 'row'), axis=0, tiled=True)  16.1 us
    all_gather x1, blocking collectives, shards(): cotangent_all = lax.all_gather(cotangent, 'src', axis=0, tiled=True)  13.5 us
    dot_general x14, matrix products, matmul_nt(): lax.dot_general(left_op, right_op, (((1,), (1,)), ((), ())), precision=la...  12 us
    dot_general x14, matrix products, matmul_tn(): lax.dot_general(left_op, right_op, (((0,), (0,)), ((), ())), precision=la...  8.24 us
    psum x1, blocking collectives, shards(): source_sum = lax.psum(source_terms, ('tile', 'row'))  5.67 us
  transfers between devices with their start and end apart: 4, of which 3 were waited for; matrix products, arithmetic and copies ran while one was open for 0% of the time, Pallas kernels for 0%

commit v1 on v0

--- a/solution.py
+++ b/solution.py
@@ -118,7 +118,25 @@
     )
     resist = jax.nn.sigmoid(STEEPNESS * (intensity - THRESHOLD))
     cotangent = LOSS_SCALE * (resist - goal_block) * STEEPNESS * resist * (1.0 - resist)
-    cotangent_all = lax.all_gather(cotangent, "src", axis=0, tiled=True)
+    length, index, rows = (lax.axis_size("src"), lax.axis_index("src"), cotangent.shape[0])
+    ahead = [(i_2, (i_2 + 1) % length) for i_2 in range(length)]
+    backward_2 = [(i_2, (i_2 - 1) % length) for i_2 in range(length)]
+    cotangent_all = jnp.zeros(
+        (*cotangent.shape[:0], length * rows, *cotangent.shape[0 + 1 :]), cotangent.dtype
+    )
+    cotangent_all = lax.dynamic_update_slice_in_dim(cotangent_all, cotangent, index * rows, axis=0)
+    from_left = from_right = cotangent
+    halfway = length // 2
+    for step in range(1, halfway + 1):
+        from_left = lax.ppermute(from_left, "src", ahead)
+        cotangent_all = lax.dynamic_update_slice_in_dim(
+            cotangent_all, from_left, (index - step) % length * rows, axis=0
+        )
+        if step < length - halfway:
+            from_right = lax.ppermute(from_right, "src", backward_2)
+            cotangent_all = lax.dynamic_update_slice_in_dim(
+                cotangent_all, from_right, (index + step) % length * rows, axis=0
+            )
     source_ids = jnp.arange(per_device, dtype=jnp.int32)
 
     def add_back(source_id, totals):

time: 179 us -> 177 us (0.989)
  blocking collectives: 35.3 us -> 21.8 us
  waiting for transfers between devices: 72.2 us -> 79.7 us
  starting transfers between devices: 4.74 us -> 8.68 us
    all_gather x1 -> x0, blocking collectives: 13.5 us -> none  [shards(): cotangent_all = lax.all_gather(cotangent, 'src', axis=0, tiled=True)]
    ppermute x0 -> x3, waiting for transfers between devices: none -> 7.48 us  [the longest x2 7.48 us: shards(): from_left = lax.ppermute(from_left, 'src', ahead)]
    ppermute x0 -> x3, starting transfers between devices: none -> 3.94 us  [the longest x1 3.7 us: shards(): from_right = lax.ppermute(from_right, 'src', backward_2)]
  transfers between devices with their start and end apart: 4 -> 7, of which waited for: 3 -> 5; matrix products, arithmetic and copies ran while one was open for 0% -> 0% of each run, Pallas kernels for 0% -> 0%
where the time goes in v1:
time: 177 us
  waiting for transfers between devices  79.7 us (45%)
  matrix products  39.2 us (22%)
  blocking collectives  21.8 us (12%)
  between operations  14.5 us (8%)
  starting transfers between devices  8.68 us (5%)
  other arithmetic  6.07 us (3%)
  local copies, waits for them, and re-layouts  4.89 us (3%)
  loops' own time  2.33 us (1%)
    psum x1, waiting for transfers between devices, shards(): grad_real, grad_imag = lax.psum((grad_real, grad_imag), ('src', 'row'))  47.7 us
    reduce_scatter x1, waiting for transfers between devices, shards(): lax.psum_scatter(jnp.sum(weights[:, None, None] * (part_real * part_real...  20.6 us
    dot_general x24, matrix products, matmul(): lax.dot_general(left_op, right_op, (((1,), (0,)), ((), ())), precision=la...  18.9 us
    all_gather x1, blocking collectives, shards(): shard_rows = lax.all_gather(window, ('src', 'row'), axis=0, tiled=True)  16.1 us
    dot_general x14, matrix products, matmul_nt(): lax.dot_general(left_op, right_op, (((1,), (1,)), ((), ())), precision=la...  12 us
    dot_general x14, matrix products, matmul_tn(): lax.dot_general(left_op, right_op, (((0,), (0,)), ((), ())), precision=la...  8.28 us
    ppermute x2, waiting for transfers between devices, shards(): from_left = lax.ppermute(from_left, 'src', ahead)  7.48 us
    psum x1, blocking collectives, shards(): source_sum = lax.psum(source_terms, ('tile', 'row'))  5.67 us
  transfers between devices with their start and end apart: 7, of which 5 were waited for; matrix products, arithmetic and copies ran while one was open for 0% of the time, Pallas kernels for 0%

profile of v1, /device:TPU:0, one launch (start us, length us, event | category | flops | bytes accessed | tf_op | source)
XLA Modules:
  0.0 177.1 jit_solution(13635740893742940535)
XLA Ops:
  7.2 16.1 %all-gather = f32[1,256,256]{2,1,0:T(8,128)S(1)} all-gather(f32[1,32,256]{2,1,0:T(8,128)} %param.9), channel_id=2, replica_groups=mesh['parts'=2,'src'=4,'tile'=2,'row'=2] {'src','row'}, dimensions={1}, use_global_device_ids=true | all-gather | bytes 294912 | tf_op jit(solution)/shard_map/all_gather | solution.py:86
  23.3 0.9 fusion.123
  24.2 0.9 convolution_negate_fusion
  29.3 1.0 fusion.152
  30.3 1.0 fusion.142
  31.3 1.0 convolution_add_fusion.3
  32.4 1.0 convolution_subtract_fusion.3
  33.6 7.3 %while.35 = (s32[]{:T(128)}, f32[3,128,256]{1,2,0:T(8,128)S(1)}, f32[3,128,256]{1,2,0:T(8,128)S(1)}, f32[3,128,256]{2,1,0:T(8,128)S(1)}, f32[3,128,256]{2,1,0:T(...) while((s32[]{:T(128)}, f32[3,128,256]{1,2,0:T(8,128)S(1)}, ...), condition=%wide.region_1.2_spmd.clone.clone, body=%wide.region_0.1_spmd.clone.clone.sunk | while | flops 202375168 | bytes 1316957 | solution.py:110
  41.8 20.6 %reduce-scatter.4.cloned.1.call-done = f32[32,256]{1,0:T(8,128)} async-done(((f32[128,256]{1,0:T(8,128)}), f32[32,256]{1,0:T(8,128)}) %reduce-scatter.4.cloned.1.call-update) | async-done | bytes 32784 | tf_op jit(solution)/shard_map/reduce_scatter | solution.py:113
  63.6 3.7 %collective-permute-start.1 = (f32[32,256]{1,0:T(8,128)S(1)}, f32[32,256]{1,0:T(8,128)S(1)}, u32[]{:S(2)}, u32[]{:S(2)}) collective-permute-start(f32[32,256]{1,0:T(8,128)S(1)} %get-tuple-element.611), channel_id=1, source_target_pairs={{0,12},{4,0},{8,4},{12,8},{1,13},{5,1},{9,5},{13,9},{2,14},{6,2},{... | collective-permute-start | bytes 98312 | tf_op jit(solution)/shard_map/ppermute | solution.py:136
  67.3 1.8 %collective-permute-done = f32[32,256]{1,0:T(8,128)S(1)} collective-permute-done((f32[32,256]{1,0:T(8,128)S(1)}, f32[32,256]{1,0:T(8,128)S(1)}, u32[]{:S(2)}, u32[]{:S(2)}) %collective-permute-start) | collective-permute-done | bytes 32800 | tf_op jit(solution)/shard_map/ppermute | solution.py:131
  69.2 5.7 %collective-permute-done.2 = f32[32,256]{1,0:T(8,128)S(1)} collective-permute-done((f32[32,256]{1,0:T(8,128)S(1)}, f32[32,256]{1,0:T(8,128)S(1)}, u32[]{:S(2)}, u32[]{:S(2)}) %collective-permute-start.2) | collective-permute-done | bytes 32800 | tf_op jit(solution)/shard_map/ppermute | solution.py:131
  74.8 26.2 %while.36 = (s32[]{:T(128)}, f32[128,128]{1,0:T(8,128)S(1)}, f32[128,128]{1,0:T(8,128)S(1)}, f32[3]{0:T(128)S(1)}, f32[3,128,128]{2,1,0:T(8,128)S(1)}, /*index=5...) while((s32[]{:T(128)}, f32[128,128]{1,0:T(8,128)S(1)}, ...), condition=%wide.region_6.7_spmd.clone.clone.clone.clone, body=%wide.region_4.6_spmd.clone.clone.clone.clone.sunk | while | flops 406126592 | bytes 4593900 | solution.py:161
  81.4 0.9 fusion.310
  88.4 0.9 fusion.308
  90.1 0.9 fusion.310
  97.1 0.8 fusion.308
  98.8 0.9 fusion.310
  101.7 5.7 %psum.23 = f32[3]{0:T(128)S(1)} all-reduce(f32[3]{0:T(128)S(1)} %get-tuple-element.296), channel_id=1, replica_groups=mesh['parts'=2,'src'=4,'tile'=2,'row'=2] {'tile','row'}, use_global_device_ids=true, to_apply=%region_9.10 | all-reduce | flops 3 | bytes 24 | tf_op jit(solution)/shard_map/psum | solution.py:165
  107.4 47.7 %all-reduce.3.cloned.1.call-done = (f32[128,128]{1,0:T(8,128)}, f32[128,128]{1,0:T(8,128)}) async-done(((f32[128,128]{1,0:T(8,128)}, f32[128,128]{1,0:T(8,128)}), (f32[128,128]{1,0:T(8,128)}, f32[128,128]{1,0:T(8,128)})) %all-reduce.3.cloned.1.call-update) | async-done | bytes 131088 | tf_op jit(solution)/shard_map/psum | solution.py:164
  155.1 1.7 fusion.150
  160.5 3.4 %collective-permute-start.3 = (f32[32,32]{1,0:T(8,128)S(1)}, f32[32,32]{1,0:T(8,128)S(1)}, u32[]{:S(2)}, u32[]{:S(2)}) collective-permute-start(f32[32,32]{1,0:T(8,128)S(1)} %get-tuple-element.619), channel_id=1, source_target_pairs={{0,2},{1,3},{4,6},{5,7},{8,10},{9,11},{12,14},{13,15},{16,18},{17,... | collective-permute-start | bytes 12296 | tf_op jit(solution)/shard_map/ppermute | solution.py:20
  163.9 1.3 collective-permute-start.4
  165.7 3.8 %collective-permute-done.4 = f32[32,32]{1,0:T(8,128)S(1)} collective-permute-done((f32[32,32]{1,0:T(8,128)S(1)}, f32[32,32]{1,0:T(8,128)S(1)}, u32[]{:S(2)}, u32[]{:S(2)}) %collective-permute-start.4) | collective-permute-done | bytes 4128 | tf_op jit(solution)/shard_map/ppermute | solution.py:23
  (111 shorter events, 38.6 us)
Async XLA Ops:
  7.2 55.2 %reduce-scatter.4.cloned.1.call-start = ((), (), s32[]{:S(2)}) async-start(), calls=%async_computation.1 | async-start | bytes 163840 | tf_op jit(solution)/shard_map/reduce_scatter | solution.py:113
  27.5 0.8 copy-start.5
  27.6 0.9 copy-start
  33.6 7.3 %copy-start.8 = (f32[3]{0:T(128)S(1)}, f32[3]{0:T(128)}, u32[]{:S(2)}) copy-start(f32[3]{0:T(128)} %param.13) | copy-start | bytes 40
  41.8 113.4 %all-reduce.3.cloned.1.call-start = ((), (), s32[]{:S(2)}) async-start(), calls=%async_computation.2 | async-start | bytes 262144 | tf_op jit(solution)/shard_map/psum | solution.py:164
  41.8 20.6 %copy-start.3 = (f32[1,32,256]{2,1,0:T(8,128)S(1)}, f32[1,32,256]{2,1,0:T(8,128)}, u32[]{:S(2)}) copy-start(f32[1,32,256]{2,1,0:T(8,128)} %param.10) | copy-start | bytes 98308
  62.4 0.8 copy-start.4
  63.2 5.9 %collective-permute-start = (f32[32,256]{1,0:T(8,128)S(1)}, f32[32,256]{1,0:T(8,128)S(1)}, u32[]{:S(2)}, u32[]{:S(2)}) collective-permute-start(f32[32,256]{1,0:T(8,128)S(1)} %get-tuple-element.611), channel_id=1, source_target_pairs={{0,4},{4,8},{8,12},{12,0},{1,5},{5,9},{9,13},{13,1},{2,6},{6,10},{... | collective-permute-start | bytes 98312 | tf_op jit(solution)/shard_map/ppermute | solution.py:131
  63.6 5.5 %collective-permute-start.1 = (f32[32,256]{1,0:T(8,128)S(1)}, f32[32,256]{1,0:T(8,128)S(1)}, u32[]{:S(2)}, u32[]{:S(2)}) collective-permute-start(f32[32,256]{1,0:T(8,128)S(1)} %get-tuple-element.611), channel_id=1, source_target_pairs={{0,12},{4,0},{8,4},{12,8},{1,13},{5,1},{9,5},{13,9},{2,14},{6,2},{... | collective-permute-start | bytes 98312 | tf_op jit(solution)/shard_map/ppermute | solution.py:136
  69.1 5.7 %collective-permute-start.2 = (f32[32,256]{1,0:T(8,128)S(1)}, f32[32,256]{1,0:T(8,128)S(1)}, u32[]{:S(2)}, u32[]{:S(2)}) collective-permute-start(f32[32,256]{1,0:T(8,128)S(1)} %collective-permute-done), channel_id=1, source_target_pairs={{0,4},{4,8},{8,12},{12,0},{1,5},{5,9},{9,13},{13,1},{2,6},{6,10},{... | collective-permute-start | bytes 98312 | tf_op jit(solution)/shard_map/ppermute | solution.py:131
  101.0 0.6 copy-start.1
  101.0 0.6 copy-start.2
  155.1 1.7 copy-start.7
  156.9 0.8 copy-start.6
  160.5 5.2 %collective-permute-start.3 = (f32[32,32]{1,0:T(8,128)S(1)}, f32[32,32]{1,0:T(8,128)S(1)}, u32[]{:S(2)}, u32[]{:S(2)}) collective-permute-start(f32[32,32]{1,0:T(8,128)S(1)} %get-tuple-element.619), channel_id=1, source_target_pairs={{0,2},{1,3},{4,6},{5,7},{8,10},{9,11},{12,14},{13,15},{16,18},{17,... | collective-permute-start | bytes 12296 | tf_op jit(solution)/shard_map/ppermute | solution.py:20
  163.9 5.6 %collective-permute-start.4 = (f32[32,32]{1,0:T(8,128)S(1)}, f32[32,32]{1,0:T(8,128)S(1)}, u32[]{:S(2)}, u32[]{:S(2)}) collective-permute-start(f32[32,32]{1,0:T(8,128)S(1)} %get-tuple-element.620), channel_id=1, source_target_pairs={{2,0},{3,1},{6,4},{7,5},{10,8},{11,9},{14,12},{15,13},{18,16},{19,... | collective-permute-start | bytes 12296 | tf_op jit(solution)/shard_map/ppermute | solution.py:23
Sparse Core Ops, SparseCore 0:
  41.9 20.4 reduce-scatter.3
  101.8 53.2 all-reduce.2
